TPU v7x, 512 devices: a whole 4x4x16 slice. The times are simulated.
512 devices in a mesh: src: 32 (over x, y, z_hi), rcv: 16 (over z_lo, core).
Axes of the slice: x: 4, y: 4, z: 16 (z_hi: 2, z_lo: 8; z = z_hi * 8 + z_lo), core: 2. Of those that a mesh axis runs over, the one named last changes fastest.
Arguments:
- observed: bfloat16 [32, 1280, 128, 128], P('src', 'rcv'), may hold values from -6 to 6
- block_row: int32 [32, 1280], P('src', 'rcv'), may hold values from 0 to 31, as said below
- block_col: int32 [32, 1280], P('src', 'rcv'), may hold values from 0 to 15
- live: int32 [32, 16], P('src', 'rcv'), may hold values from 20 to 80, as said below
- row_factor: bfloat16 [131072, 64], P('src'), may hold values from -5 to 5
- col_factor: bfloat16 [32768, 64], P('rcv'), may hold values from -5 to 5
Outputs:
- new_rows: bfloat16 [131072, 64], P('src')
- new_cols: bfloat16 [32768, 64], P('rcv')
Inputs may be any that keep to these rules, and one draw needn't show every extreme that they name: `block_row`: within one device the 80 slots name distinct blocks of its tile. `live`: some device has all 80 slots in use.
All inputs are finite; a program needn't handle non-finite values.
Results may differ from a plain program's by a relative error of at most 0.007.
Values may be sent and summed in bfloat16 or wider, within the bound.
A program may use at most 64 MiB of HBM per device.

v0:
```python
import math
import jax
import jax.numpy as jnp
from jax import lax
from jax.sharding import PartitionSpec as P


def local(observed, block_row, block_col, live, row_factor, col_factor):
    slot_data = observed[0]
    slot_total = slot_data.shape[0]
    block_size = slot_data.shape[1]
    rank_width = row_factor.shape[1]
    row_block_total = row_factor.shape[0] // block_size
    col_block_total = col_factor.shape[0] // block_size
    row_table = row_factor.reshape(row_block_total, block_size, rank_width)
    col_table = col_factor.reshape(col_block_total, block_size, rank_width)
    row_pick = block_row[0][:, None] == jnp.arange(row_block_total, dtype=jnp.int32)[None, :]
    col_pick = block_col[0][:, None] == jnp.arange(col_block_total, dtype=jnp.int32)[None, :]
    row_blocks = jnp.einsum(
        "ks,sar->kar", row_pick.astype(jnp.bfloat16), row_table, preferred_element_type=jnp.float32
    ).astype(jnp.bfloat16)
    col_blocks = jnp.einsum(
        "kc,cbr->kbr", col_pick.astype(jnp.bfloat16), col_table, preferred_element_type=jnp.float32
    ).astype(jnp.bfloat16)
    predicted = jnp.einsum(
        "kar,kbr->kab", row_blocks, col_blocks, preferred_element_type=jnp.float32
    )
    slot_live = jnp.arange(slot_total, dtype=jnp.int32) < live[0, 0]
    residual = jnp.where(
        slot_live[:, None, None], predicted - slot_data.astype(jnp.float32), 0.0
    ).astype(jnp.bfloat16)
    row_terms = jnp.einsum("kab,kbr->kar", residual, col_blocks, preferred_element_type=jnp.float32)
    row_grad = jnp.einsum("ks,kar->sar", row_pick.astype(jnp.float32), row_terms).reshape(
        row_block_total * block_size, rank_width
    )
    row_step = 0.5 / math.sqrt(slot_total * block_size * lax.axis_size("rcv") // row_block_total)
    row_sums = lax.psum(row_grad, "rcv")
    new_rows = (0.9 * row_factor.astype(jnp.float32) - row_step * row_sums).astype(jnp.bfloat16)
    col_terms = jnp.einsum("kab,kar->kbr", residual, row_blocks, preferred_element_type=jnp.float32)
    col_grad = jnp.einsum("kc,kbr->cbr", col_pick.astype(jnp.float32), col_terms).reshape(
        col_block_total * block_size, rank_width
    )
    col_step = 0.5 / math.sqrt(slot_total * block_size * lax.axis_size("src") // col_block_total)
    col_sums = lax.psum(col_grad, "src")
    new_cols = (0.9 * col_factor.astype(jnp.float32) - col_step * col_sums).astype(jnp.bfloat16)
    return (new_rows, new_cols)


def solution(mesh):
    return jax.shard_map(
        local,
        mesh=mesh,
        in_specs=(
            P("src", "rcv", None, None),
            P("src", "rcv"),
            P("src", "rcv"),
            P("src", "rcv"),
            P("src", None),
            P("rcv", None),
        ),
        out_specs=(P("src", None), P("rcv", None)),
        check_vma=False,
    )
```

profile of v0, /device:TPU:1, one launch (start us, length us, event | category | flops | bytes accessed | tf_op | source)
XLA Modules:
  0.0 812.5 jit_solution(6672184415892702241)
XLA Ops:
  7.2 0.0 all-reduce.5.cloned.1.call-start
  7.9 1.0 copy.13
  8.9 0.0 copy-start.3
  8.9 1.1 copy.12
  10.0 0.0 copy-start.5
  10.1 0.5 convolution_convert_fusion.1
  10.6 0.5 convolution_convert_fusion
  11.2 0.6 copy-done.5
  11.8 1.6 fusion.1
  13.4 0.0 copy-done
  13.4 0.8 fusion.9
  14.2 0.8 fusion.2
  15.1 1.0 copy.31
  16.0 0.0 all-reduce.5.cloned.1.call-update
  16.0 0.0 all-reduce.3.cloned.1.call-start
  16.1 3.2 fusion.6
  19.3 0.9 fusion.4
  20.2 0.0 copy-start.2
  20.2 1.6 copy.30
  21.9 0.0 all-reduce.3.cloned.1.call-update
  21.9 558.6 %all-reduce.5.cloned.1.call-done = f32[2048,64]{0,1:T(8,128)} async-done(((f32[2048,64]{0,1:T(8,128)}), f32[2048,64]{0,1:T(8,128)}) %all-reduce.5.cloned.1.call-update) | async-done | bytes 524304 | tf_op jit(solution)/shard_map/psum | solution.py:44
  580.5 1.8 subtract_convert_fusion.1
  582.3 221.1 %all-reduce.3.cloned.1.call-done = f32[4096,64]{0,1:T(8,128)} async-done(((f32[4096,64]{0,1:T(8,128)}), f32[4096,64]{0,1:T(8,128)}) %all-reduce.3.cloned.1.call-update) | async-done | bytes 1048592 | tf_op jit(solution)/shard_map/psum | solution.py:37
  803.5 2.2 subtract_convert_fusion
  (8 shorter events, 0.0 us)
Async XLA Ops:
  7.2 2.9 copy-start.4
  7.2 573.3 %all-reduce.5.cloned.1.call-start = ((), (), s32[]{:S(2)}) async-start(), calls=%async_computation.1 | async-start | bytes 1048576 | tf_op jit(solution)/shard_map/psum | solution.py:44
  8.9 1.7 copy-start.3
  10.0 1.7 copy-start.5
  11.8 1.6 copy-start
  16.0 787.5 %all-reduce.3.cloned.1.call-start = ((), (), s32[]{:S(2)}) async-start(), calls=%async_computation | async-start | bytes 2097152 | tf_op jit(solution)/shard_map/psum | solution.py:37
  20.2 560.3 %copy-start.2 = (bf16[2048,64]{0,1:T(8,128)(2,1)S(1)}, bf16[2048,64]{0,1:T(8,128)(2,1)}, u32[]{:S(2)}) copy-start(bf16[2048,64]{0,1:T(8,128)(2,1)} %param.11) | copy-start | bytes 786436
  21.9 781.6 %copy-start.1 = (bf16[4096,64]{0,1:T(8,128)(2,1)S(1)}, bf16[4096,64]{0,1:T(8,128)(2,1)}, u32[]{:S(2)}) copy-start(bf16[4096,64]{0,1:T(8,128)(2,1)} %param.10) | copy-start | bytes 1572868
Sparse Core Ops, SparseCore 0:
  16.2 564.3 all-reduce.4
  583.4 220.0 all-reduce.2
where the time goes:
time: 813 us
  waiting for transfers between devices  780 us (96%)
  between operations  14.8 us (2%)
  matrix products  8.45 us (1%)
    psum x1, waiting for transfers between devices, local(): col_sums = lax.psum(col_grad, 'src')  559 us
    psum x1, waiting for transfers between devices, local(): row_sums = lax.psum(row_grad, 'rcv')  221 us
  transfers between devices with their start and end apart: 2, of which 2 were waited for; matrix products, arithmetic and copies ran while one was open for 1% of the time, Pallas kernels for 0%

commit v1 on v0

--- a/solution.py
+++ b/solution.py
@@ -41,7 +41,7 @@
         col_block_total * block_size, rank_width
     )
     col_step = 0.5 / math.sqrt(slot_total * block_size * lax.axis_size("src") // col_block_total)
-    col_sums = lax.psum(col_grad, "src")
+    col_sums = jnp.sum(lax.all_gather(col_grad, "src"), axis=0)
     new_cols = (0.9 * col_factor.astype(jnp.float32) - col_step * col_sums).astype(jnp.bfloat16)
     return (new_rows, new_cols)
 

time: 813 us -> 541 us (0.67)
  waiting for transfers between devices: 780 us -> 500 us
    psum x1 -> x0, waiting for transfers between devices: 559 us -> none  [local(): col_sums = lax.psum(col_grad, 'src')]
    psum x1, waiting for transfers between devices: 221 us -> 500 us  [local(): row_sums = lax.psum(row_grad, 'rcv')]
  transfers between devices with their start and end apart: 2 -> 2, of which waited for: 2 -> 1; matrix products, arithmetic and copies ran while one was open for 1% -> 1% of each run, Pallas kernels for 0% -> 0%
where the time goes in v1:
time: 541 us
  waiting for transfers between devices  500 us (92%)
  between operations  16.2 us (3%)
  other arithmetic  9.89 us (2%)
  matrix products  8.45 us (2%)
  local copies, waits for them, and re-layouts  5.76 us (1%)
    psum x1, waiting for transfers between devices, local(): row_sums = lax.psum(row_grad, 'rcv')  500 us
  transfers between devices with their start and end apart: 2, of which 1 were waited for; matrix products, arithmetic and copies ran while one was open for 1% of the time, Pallas kernels for 0%

profile of v1, /device:TPU:1, one launch (start us, length us, event | category | flops | bytes accessed | tf_op | source)
XLA Modules:
  0.0 540.7 jit_solution(9294850651390814022)
XLA Ops:
  8.0 0.0 all-reduce.2.cloned.1.call-start
  8.7 1.0 copy.15
  9.7 0.0 copy-start.3
  9.7 1.1 copy.14
  10.9 0.0 copy-start.5
  10.9 0.5 convolution_convert_fusion
  11.4 0.5 convolution_convert_fusion.1
  12.0 1.1 copy-done
  13.1 0.0 copy-done.5
  13.1 1.6 fusion.1
  14.7 1.9 fusion.6
  16.6 0.9 fusion.4
  17.5 1.6 copy.30
  19.2 0.0 all-reduce.2.cloned.1.call-update
  19.2 0.0 all-gather.2.cloned.1.call-start
  19.2 2.1 fusion.9
  21.4 0.0 copy-start.1
  21.4 0.8 fusion.2
  22.2 0.9 all_gather_reshape.3
  23.1 0.0 all-gather.2.cloned.1.call-update
  23.1 500.3 %all-reduce.2.cloned.1.call-done = f32[4096,64]{0,1:T(8,128)} async-done(((f32[4096,64]{0,1:T(8,128)}), f32[4096,64]{0,1:T(8,128)}) %all-reduce.2.cloned.1.call-update) | async-done | bytes 1048592 | tf_op jit(solution)/shard_map/psum | solution.py:37
  523.4 2.2 subtract_convert_fusion
  525.5 6.9 %reduce_sum.9 = f32[2048,64]{0,1:T(8,128)S(1)} reduce(f32[32,2048,64]{1,2,0:T(8,128)} %all-gather.2.cloned.1.call-done, f32[]{:T(128)} %constant.0.clone.1), dimensions={0}, to_apply=%region_1.2 | reduce | flops 4063232 | bytes 17301508 | tf_op jit(solution)/shard_map/reduce_sum | solution.py:44
  532.5 0.8 subtract_convert_fusion.1
  (9 shorter events, 0.0 us)
Async XLA Ops:
  8.0 2.9 copy-start.4
  8.0 515.4 %all-reduce.2.cloned.1.call-start = ((), (), s32[]{:S(2)}) async-start(), calls=%async_computation | async-start | bytes 2097152 | tf_op jit(solution)/shard_map/psum | solution.py:37
  9.7 1.7 copy-start.3
  10.9 2.2 copy-start.5
  12.0 1.1 copy-start
  19.2 506.4 %all-gather.2.cloned.1.call-start = ((), (), s32[]{:S(2)}) async-start(), calls=%async_computation.1 | async-start | bytes 17301504 | tf_op jit(solution)/shard_map/all_gather | solution.py:44
  21.4 502.0 %copy-start.1 = (bf16[4096,64]{0,1:T(8,128)(2,1)S(1)}, bf16[4096,64]{0,1:T(8,128)(2,1)}, u32[]{:S(2)}) copy-start(bf16[4096,64]{0,1:T(8,128)(2,1)} %param.10) | copy-start | bytes 1572868
  525.5 6.9 %copy-start.2 = (bf16[2048,64]{0,1:T(8,128)(2,1)S(1)}, bf16[2048,64]{0,1:T(8,128)(2,1)}, u32[]{:S(2)}) copy-start(bf16[2048,64]{0,1:T(8,128)(2,1)} %param.11) | copy-start | bytes 786436
Sparse Core Ops, SparseCore 0:
  19.3 504.0 all-reduce.1
Sparse Core Ops, SparseCore 1:
  24.0 427.9 all-gather.1
